TPU v7x, 32 devices: a whole 2x2x4 slice. The times are simulated.
32 devices in a mesh: ep: 4 (over z), fsdp: 4 (over y, x), copy: 2 (over core).
Axes of the slice: x: 2, y: 2, z: 4, core: 2. Of those that a mesh axis runs over, the one named last changes fastest.
Arguments:
- master_down: float32 [128, 1408, 2048], P(('copy', 'ep'), None, 'fsdp'), parts along dimension 0, may hold values from -0.21875 to 0.21875
- second_down: bfloat16 [128, 1408, 2048], P(('copy', 'ep'), None, 'fsdp'), parts along dimension 0, may hold values from -0.078125 to 0.078125
- router_weight: float32 [4096, 64], P(('copy', 'fsdp'), 'ep'), parts along dimension 0, may hold values from -0.125 to 0.125
- router_gain: float32 [4096], P(('copy', 'fsdp')), parts along dimension 0, may hold values from 0.25 to 1.75
Outputs:
- final_down: bfloat16 [128, 1408, 2048], P(('copy', 'ep')), parts along dimension 0
- scale_down: float32 [128, 1408], P(('copy', 'ep')), parts along dimension 0
- serve_router: bfloat16 [4096, 64], P('copy'), parts along dimension 0
There are 2 independent parts, one for each index of `copy`. A program takes and returns all parts, laid end to end along the dimension named above; each array names one. Nothing has to cross between parts.
All inputs are finite; a program needn't handle non-finite values. Where the computation divides by a largest or mean magnitude, that divisor is 1e-20 or more.
Results may differ from a plain program's by a relative error of at most 0.001.
Values may be sent and summed in bfloat16 or wider, within the bound.
A program may use at most 320 MiB of HBM per device.

v0:
```python
import jax
import jax.numpy as jnp
from jax import lax
from jax.sharding import PartitionSpec as P

D_MODEL = 2048


def on_device(master_down, second_down, router_weight, router_gain):
    merged_down = master_down + second_down.astype(jnp.float32)
    total_down = lax.psum(jnp.sum(jnp.abs(merged_down), axis=2), "fsdp")
    scale_down = total_down / D_MODEL
    narrow_down = (merged_down / jnp.expand_dims(scale_down, 2)).astype(jnp.bfloat16)
    final_down = lax.all_gather(narrow_down, "fsdp", axis=2, tiled=True)
    part_router = (router_weight * router_gain[:, None]).astype(jnp.bfloat16)
    row_router = lax.all_gather(part_router, "fsdp", axis=0, tiled=True)
    serve_router = lax.all_gather(row_router, "ep", axis=1, tiled=True)
    return (final_down, scale_down, serve_router)


def solution(mesh):
    return jax.shard_map(
        on_device,
        mesh=mesh,
        in_specs=(
            P(("copy", "ep"), None, "fsdp"),
            P(("copy", "ep"), None, "fsdp"),
            P(("copy", "fsdp"), "ep"),
            P(("copy", "fsdp")),
        ),
        out_specs=(P(("copy", "ep"), None, None), P(("copy", "ep"), None), P("copy", None)),
        check_vma=False,
    )
```

profile of v0, /device:TPU:0, one launch (start us, length us, event | category | flops | bytes accessed | tf_op | source)
XLA Modules:
  0.0 960.5 jit_solution(3699545741664936519)
XLA Ops:
  7.2 0.0 all-reduce.2.cloned.1.call-start
  7.2 22.3 %abs_reduce_fusion = f32[16,1408]{1,0:T(8,128)} fusion(f32[16,1408,512]{2,1,0:T(8,128)} %param.4, bf16[16,1408,512]{2,1,0:T(8,128)(2,1)} %param.5), kind=kLoop, calls=%fused_computation.1 | loop fusion | flops 46114816 | bytes 69296128 | tf_op jit(solution)/shard_map/reduce_sum | solution.py:11
  29.5 0.0 all-reduce.2.cloned.1.call-update
  29.5 0.0 all-gather.2.cloned.1.call-start
  29.6 44.8 %all-reduce.2.cloned.1.call-done = f32[16,1408]{1,0:T(8,128)} async-done(((f32[16,1408]{1,0:T(8,128)}), f32[16,1408]{1,0:T(8,128)}) %all-reduce.2.cloned.1.call-update) | async-done | bytes 90128 | tf_op jit(solution)/shard_map/psum | solution.py:11
  74.4 0.9 broadcast_multiply_fusion
  75.3 0.0 copy-start
  75.3 0.0 copy-start.1
  75.3 0.0 copy-start.2
  75.3 30.5 %divide_convert_fusion = bf16[16,1408,512]{2,1,0:T(8,128)(2,1)} fusion(f32[16,1408,512]{2,1,0:T(8,128)} %param.4, bf16[16,1408,512]{2,1,0:T(8,128)(2,1)} %param.5, f32[16,1408]{1,0:T(8,128)S(1)} %broadcast_multiply_fusion), kind=kLoop, calls=%fused_computation | loop fusion | flops 46137344 | bytes 92364800 | tf_op jit(solution)/shard_map/convert_element_type | solution.py:13
  105.8 0.0 copy-done
  105.9 0.0 all-gather.2.cloned.1.call-update
  105.9 0.0 copy-done.1
  105.9 0.0 copy-done.2
  105.9 8.2 all_gather.10
  114.1 14.5 %all_gather.11 = bf16[2048,64]{0,1:T(8,128)(2,1)S(1)} all-gather(bf16[2048,16]{0,1:T(8,128)(2,1)S(1)} %all_gather.10), channel_id=1, replica_groups=mesh['ep'=4,'fsdp'=4,'copy'=2] {'ep'}, dimensions={1}, use_global_device_ids=true | all-gather | bytes 327680 | tf_op jit(solution)/shard_map/all_gather | solution.py:17
  128.7 764.0 %all-gather.2.cloned.1.call-done = bf16[16,1408,2048]{2,1,0:T(8,128)(2,1)} async-done(((bf16[16,1408,512]{2,1,0:T(8,128)(2,1)}), bf16[16,1408,2048]{2,1,0:T(8,128)(2,1)}) %all-gather.2.cloned.1.call-update) | async-done | bytes 92274704 | tf_op jit(solution)/shard_map/all_gather | solution.py:14
  892.7 60.3 %copy.10 = bf16[16,1408,2048]{2,1,0:T(8,128)(2,1)} copy(bf16[16,1408,2048]{2,1,0:T(8,128)(2,1)} %all-gather.2.cloned.1.call-done) | data formatting | bytes 184549376
  953.0 0.7 copy.11
  (1 shorter events, 0.0 us)
Async XLA Ops:
  7.2 67.3 %all-reduce.2.cloned.1.call-start = ((), (), s32[]{:S(2)}) async-start(), calls=%async_computation | async-start | bytes 180224 | tf_op jit(solution)/shard_map/psum | solution.py:11
  29.5 863.2 %all-gather.2.cloned.1.call-start = ((), (), s32[]{:S(2)}) async-start(), calls=%async_computation.1 | async-start | bytes 115343360 | tf_op jit(solution)/shard_map/all_gather | solution.py:14
  75.3 30.5 %copy-start = (f32[16,1408]{1,0:T(8,128)}, f32[16,1408]{1,0:T(8,128)S(1)}, u32[]{:S(2)}) copy-start(f32[16,1408]{1,0:T(8,128)S(1)} %broadcast_multiply_fusion) | copy-start | bytes 270340
  75.3 30.6 %copy-start.1 = (f32[512,16]{0,1:T(8,128)S(1)}, f32[512,16]{0,1:T(8,128)}, u32[]{:S(2)}) copy-start(f32[512,16]{0,1:T(8,128)} %param.6) | copy-start | bytes 98308
  75.3 30.6 %copy-start.2 = (f32[512]{0:T(512)S(1)}, f32[512]{0:T(512)}, u32[]{:S(2)}) copy-start(f32[512]{0:T(512)} %param.7) | copy-start | bytes 6148
Sparse Core Ops, SparseCore 0:
  29.7 44.7 all-reduce.1
  106.0 786.6 all-gather.1
where the time goes:
time: 961 us
  waiting for transfers between devices  809 us (84%)
  local copies, waits for them, and re-layouts  61 us (6%)
  other arithmetic  53.7 us (6%)
  blocking collectives  22.7 us (2%)
  between operations  14.1 us (1%)
    all_gather x1, waiting for transfers between devices, on_device(): final_down = lax.all_gather(narrow_down, 'fsdp', axis=2, tiled=True)  764 us
    unnamed x8, local copies, waits for them, and re-layouts  61 us
    psum x1, waiting for transfers between devices, on_device(): total_down = lax.psum(jnp.sum(jnp.abs(merged_down), axis=2), 'fsdp')  44.8 us
    convert_element_type x1, other arithmetic, on_device(): (merged_down / jnp.expand_dims(scale_down, 2)).astype(jnp.bfloat16)  30.5 us
    reduce_sum x1, other arithmetic, on_device(): total_down = lax.psum(jnp.sum(jnp.abs(merged_down), axis=2), 'fsdp')  22.3 us
  transfers between devices with their start and end apart: 2, of which 2 were waited for; matrix products, arithmetic and copies ran while one was open for 0% of the time, Pallas kernels for 0%

commit v1 on v0

v1 whole, which is shorter than its diff:
```python
import jax
import jax.numpy as jnp
from jax import lax
from jax.experimental import pallas as pl
from jax.experimental.pallas import tpu as pltpu
from jax.sharding import PartitionSpec as P


def pieces_of(experts):
    if experts < 8:
        return [experts]
    end = experts // 16 or 1
    return [end, experts - 2 * end, end]


def rows_per_block(rows):
    return max(r for r in range(16, min(rows, 1024) + 1, 16) if rows % r == 0)


def put_first(piece_ref, out_ref):
    out_ref[...] = piece_ref[...]


def put_next(piece_ref, whole_ref, out_ref):
    out_ref[...] = piece_ref[...]


def put(whole, piece, at, experts):
    count, rows, width = piece.shape
    block = rows_per_block(rows)
    spec = pl.BlockSpec((1, block, width), lambda e, r: (e, r, 0))
    first = whole is None
    return pl.pallas_call(
        put_first if first else put_next,
        grid=(count, rows // block),
        in_specs=[spec] if first else [spec, pl.BlockSpec(memory_space=pl.ANY)],
        out_specs=pl.BlockSpec((1, block, width), lambda e, r: (e + at, r, 0)),
        out_shape=jax.ShapeDtypeStruct((experts, rows, width), piece.dtype),
        input_output_aliases={} if first else {1: 0},
        cost_estimate=pl.CostEstimate(flops=0, bytes_accessed=2 * piece.size * piece.dtype.itemsize, transcendentals=0),
        name=f"put_{at}",
    )(*((piece,) if first else (piece, whole)))


def on_device(master_down, second_down, router_weight, router_gain):
    experts, _, width = master_down.shape
    d_model = width * lax.axis_size("fsdp")

    def merged(at, count):
        return master_down[at : at + count] + second_down[at : at + count].astype(jnp.float32)

    def scale(at, count):
        part = jnp.sum(jnp.abs(merged(at, count)), axis=2)
        return jnp.sum(lax.all_gather(part, "fsdp", axis=0), axis=0) / d_model

    def gathered(at, count, scale):
        narrow = (merged(at, count) / scale[:, :, None]).astype(jnp.bfloat16)
        return lax.all_gather(narrow, "fsdp", axis=2, tiled=True)

    pieces = pieces_of(experts)
    first = pieces[0]
    scales = [scale(0, first)]
    if experts > first:
        scales.append(scale(first, experts - first))
    scale_down = jnp.concatenate(scales, axis=0)

    blocks, at = [], 0
    for number, count in enumerate(pieces):
        own = scales[0] if number == 0 else scales[1][at - first : at - first + count]
        blocks.append((at, gathered(at, count, own)))
        at += count

    part_router = (router_weight * router_gain[:, None]).astype(jnp.bfloat16)
    row_router = lax.all_gather(part_router, "fsdp", axis=0, tiled=True)
    serve_router = lax.all_gather(row_router, "ep", axis=1, tiled=True)

    final_down = None
    for at, block in blocks:
        final_down = put(final_down, block, at, experts)
    return (final_down, scale_down, serve_router)


def solution(mesh):
    return jax.shard_map(
        on_device,
        mesh=mesh,
        in_specs=(
            P(("copy", "ep"), None, "fsdp"),
            P(("copy", "ep"), None, "fsdp"),
            P(("copy", "fsdp"), "ep"),
            P(("copy", "fsdp")),
        ),
        out_specs=(P(("copy", "ep"), None, None), P(("copy", "ep"), None), P("copy", None)),
        check_vma=False,
    )
```

time: 961 us -> 893 us (0.929)
  waiting for transfers between devices: 809 us -> 711 us
  Pallas kernels: 0 us -> 69 us
  local copies, waits for them, and re-layouts: 61 us -> 0.75 us
  blocking collectives: 22.7 us -> 41.4 us
    pallas_call x0 -> x3, Pallas kernels: none -> 69 us  [put(): pl.pallas_call(put_first if first else put_next, grid=(count, rows // blo...]
    unnamed x8, local copies, waits for them, and re-layouts: 61 us -> 0.72 us
    all_gather x1 -> x3, waiting for transfers between devices: 764 us -> 710 us  [gathered(): return lax.all_gather(narrow, 'fsdp', axis=2, tiled=True)]
    psum x1 -> x0, waiting for transfers between devices: 44.8 us -> none  [on_device(): total_down = lax.psum(jnp.sum(jnp.abs(merged_down), axis=2), 'fsdp')]
    all_gather x0 -> x2, blocking collectives: none -> 19 us  [scale(): return jnp.sum(lax.all_gather(part, 'fsdp', axis=0), axis=0) / d_model]
    convert_element_type x1 -> x2, other arithmetic: 30.5 us -> 32.4 us  [gathered(): narrow = (merged(at, count) / scale[:, :, None]).astype(jnp.bfloat16)]
    reduce_sum x1 -> x4, other arithmetic: 22.3 us -> 23.7 us  [the longest x2 23.6 us: scale(): part = jnp.sum(jnp.abs(merged(at, count)), axis=2)]
  transfers between devices with their start and end apart: 2 -> 3, of which waited for: 2 -> 3; matrix products, arithmetic and copies ran while one was open for 0% -> 3% of each run, Pallas kernels for 0% -> 7%
where the time goes in v1:
time: 893 us; the launch traced here: 892 us
  waiting for transfers between devices  711 us (80%)
  Pallas kernels  69 us (8%)
  other arithmetic  56.7 us (6%)
  blocking collectives  41.4 us (5%)
  between operations  13.8 us (2%)
    all_gather x3, waiting for transfers between devices, gathered(): return lax.all_gather(narrow, 'fsdp', axis=2, tiled=True)  710 us
    pallas_call x3, Pallas kernels, put(): pl.pallas_call(put_first if first else put_next, grid=(count, rows // blo...  69 us
    convert_element_type x2, other arithmetic, gathered(): narrow = (merged(at, count) / scale[:, :, None]).astype(jnp.bfloat16)  32.4 us
    reduce_sum x2, other arithmetic, scale(): part = jnp.sum(jnp.abs(merged(at, count)), axis=2)  23.6 us
    all_gather x2, blocking collectives, scale(): return jnp.sum(lax.all_gather(part, 'fsdp', axis=0), axis=0) / d_model  19 us
  transfers between devices with their start and end apart: 3, of which 3 were waited for; matrix products, arithmetic and copies ran while one was open for 3% of the time, Pallas kernels for 7%

profile of v1, /device:TPU:0, one launch (start us, length us, event | category | flops | bytes accessed | tf_op | source)
XLA Modules:
  0.0 892.4 jit_solution(3948425720945479675)
XLA Ops:
  7.2 0.0 all-gather.12.cloned.1.call-start
  7.2 21.0 %abs_reduce_fusion = f32[15,1408]{1,0:T(8,128)S(1)} fusion(f32[16,1408,512]{2,1,0:T(8,128)} %param.4, bf16[16,1408,512]{2,1,0:T(8,128)(2,1)} %param.5), kind=kLoop, calls=%fused_computation | loop fusion | flops 43232640 | bytes 64965120 | tf_op jit(solution)/shard_map/reduce_sum | solution.py:53
  28.2 2.7 abs_reduce_fusion.1
  30.8 10.9 %all-gather.2 = f32[4,15,1408]{2,1,0:T(8,128)S(1)} all-gather(f32[1,15,1408]{2,1,0:T(8,128)S(1)} %bitcast.3), channel_id=2, replica_groups=mesh['ep'=4,'fsdp'=4,'copy'=2] {'fsdp'}, dimensions={0}, use_global_device_ids=true | all-gather | bytes 422400 | tf_op jit(solution)/shard_map/all_gather | solution.py:54
  41.8 8.2 all-gather.3
  50.0 5.1 divide_convert_fusion.1
  55.1 0.0 all-gather.12.cloned.1.call-update
  55.1 0.0 all-gather.10.cloned.1.call-start
  55.2 27.3 %divide_convert_fusion = bf16[14,1408,512]{2,1,0:T(8,128)(2,1)} fusion(f32[16,1408,512]{2,1,0:T(8,128)} %param.4, f32[14,1408]{1,0:T(8,128)S(1)} %bitcast.2, bf16[16,1408,512]{2,1,0:T(8,128)(2,1)} %param.5), kind=kLoop, calls=%fused_computation.1 | loop fusion | flops 40370176 | bytes 80819200 | tf_op jit(solution)/shard_map/convert_element_type | solution.py:57
  82.5 0.0 copy-start.1
  82.5 0.0 copy-start.2
  82.5 0.0 all-gather.10.cloned.1.call-update
  82.5 0.0 all-gather.8.cloned.1.call-start
  82.5 0.7 all-gather.8.cloned.1.call-update
  83.2 0.0 copy-done.1
  83.3 0.0 copy-done.2
  83.3 7.5 all_gather.34
  90.8 14.9 %all_gather.35 = bf16[2048,64]{0,1:T(8,128)(2,1)} all-gather(bf16[2048,16]{0,1:T(8,128)(2,1)S(1)} %all_gather.34), channel_id=1, replica_groups=mesh['ep'=4,'fsdp'=4,'copy'=2] {'ep'}, dimensions={1}, use_global_device_ids=true | all-gather | bytes 327680 | tf_op jit(solution)/shard_map/all_gather | solution.py:75
  105.7 0.7 pad_maximum_fusion
  106.4 14.9 %all-gather.12.cloned.1.call-done.piece_ref = bf16[1,1408,2048]{2,1,0:T(8,128)(2,1)} async-done(((bf16[1,1408,512]{2,1,0:T(8,128)(2,1)}), bf16[1,1408,2048]{2,1,0:T(8,128)(2,1)}) %all-gather.12.cloned.1.call-update) | async-done | bytes 5767184 | tf_op jit(solution)/shard_map/all_gather | solution.py:58
  121.3 4.5 put_0.1.whole_ref
  125.8 687.5 %all-gather.10.cloned.1.call-done.piece_ref = bf16[14,1408,2048]{2,1,0:T(8,128)(2,1)} async-done(((bf16[14,1408,512]{2,1,0:T(8,128)(2,1)}), bf16[14,1408,2048]{2,1,0:T(8,128)(2,1)}) %all-gather.10.cloned.1.call-update) | async-done | bytes 80740368 | tf_op jit(solution)/shard_map/all_gather | solution.py:58
  813.3 60.0 %put_1.1.whole_ref = bf16[16,1408,2048]{2,1,0:T(8,128)(2,1)} custom-call(bf16[14,1408,2048]{2,1,0:T(8,128)(2,1)} %all-gather.10.cloned.1.call-done.piece_ref, bf16[16,1408,2048]{2,1,0:T(8,128)(2,1)} %put_0.1.whole_ref), custom_call_target="tpu_custom_call", output_to_operand_aliasing={{}: (1, {})} | custom-call | bytes 161480704 | tf_op jit(solution)/shard_map/put_1/pallas_call | solution.py:33
  873.2 0.0 copy-start
  873.2 7.4 all-gather.8.cloned.1.call-done.piece_ref
  880.7 4.5 put_15.1
  885.2 0.0 copy-done
  885.2 0.7 copy.12
  (8 shorter events, 0.1 us)
Async XLA Ops:
  7.2 114.1 %all-gather.12.cloned.1.call-start = ((), (), s32[]{:S(2)}) async-start(), calls=%async_computation.2 | async-start | bytes 7208960 | tf_op jit(solution)/shard_map/all_gather | solution.py:58
  55.1 758.1 %all-gather.10.cloned.1.call-start = ((), (), s32[]{:S(2)}) async-start(), calls=%async_computation.1 | async-start | bytes 100925440 | tf_op jit(solution)/shard_map/all_gather | solution.py:58
  82.5 0.8 copy-start.1
  82.5 0.8 copy-start.2
  82.5 798.2 %all-gather.8.cloned.1.call-start = ((), (), s32[]{:S(2)}) async-start(), calls=%async_computation | async-start | bytes 7208960 | tf_op jit(solution)/shard_map/all_gather | solution.py:58
  873.2 12.0 %copy-start = (bf16[2048,64]{0,1:T(8,128)(2,1)S(1)}, bf16[2048,64]{0,1:T(8,128)(2,1)}, u32[]{:S(2)}) copy-start(bf16[2048,64]{0,1:T(8,128)(2,1)} %all_gather.35) | copy-start | bytes 786436
Sparse Core Ops, SparseCore 0:
  55.2 65.9 all-gather.11
  123.1 690.1 all-gather.9
  815.1 65.5 all-gather.7
